TPU v7x, 32 devices: a whole 2x2x4 slice. The times are simulated.
32 devices in a mesh: tm: 4 (over x, core), row: 2 (over y), col: 4 (over z).
Axes of the slice: x: 2, y: 2, z: 4, core: 2. Of those that a mesh axis runs over, the one named last changes fastest.
Arguments:
- first_inverse: bfloat16 [4, 1536, 1536], P('tm', ('row', 'col')), as said below
- second_diag: bfloat16 [4, 1536, 1536], P('tm', ('row', 'col')), as said below
- coupling: bfloat16 [4, 3, 1536, 1536], P('tm', None, ('row', 'col'))
- arrow_rows: float32 [4, 2, 8, 1536], P('tm')
- tip_block: float32 [8, 8], replicated, may hold values from -6 to 6
Outputs:
- separator_update: float32 [4, 1536, 1536], P('tm', ('row', 'col'))
- separator_fill: float32 [4, 1536, 1536], P('tm', ('row', 'col'))
- reduced_tip: float32 [8, 8], replicated
Inputs may be any that keep to these rules, and one draw needn't show every extreme that they name: For every p, first_inverse[p] is lower triangular with a positive diagonal. For every p, second_diag[p] is symmetric, and second_diag[p] minus coupling[p, 1] first_inverse[p]^T first_inverse[p] coupling[p, 1]^T is positive definite.
All inputs are finite; a program needn't handle non-finite values.
Results may differ from a plain program's by a relative error of at most 0.009.
Values may be sent and summed in bfloat16 or wider, within the bound.
No kernel may reach another device: no remote copies, remote signals or barrier semaphores. Data moves between devices by JAX's collectives and lax.ppermute only.
A program may use at most 128 MiB of HBM per device.

v0:
```python
import jax
import jax.numpy as jnp
from jax import lax
from jax.sharding import PartitionSpec as P


def from_behind(block, axis, distance):
    devices = range(lax.axis_size(axis))
    route = [(i - distance, i) for i in devices if i - distance in devices]
    return lax.ppermute(block, axis, route)


def right_solve(factor, rhs_rows):
    return lax.linalg.triangular_solve(
        factor, rhs_rows, left_side=False, lower=True, transpose_a=True
    )


def outer_rows(left_rows, right_rows):
    return jnp.einsum("ik,jk->ij", left_rows, right_rows, preferred_element_type=jnp.float32)


def gather_block(one_share):
    return lax.all_gather(one_share, ("row", "col"), axis=0, tiled=True)


def spread_panels(first_panel, second_panel):
    return (
        lax.all_gather(first_panel, ("row", "col"), axis=0, tiled=True),
        lax.all_gather(second_panel, ("row", "col"), axis=0, tiled=True),
    )


def shards(first_inverse, second_diag, coupling, arrow_rows, tip_block):
    share = coupling.shape[2]
    inverse_whole = gather_block(first_inverse[0])
    rhs_first = jnp.concatenate([coupling[0, 0], coupling[0, 1]], axis=0)
    solved_first = outer_rows(rhs_first, inverse_whole)
    top_own = solved_first[:share].astype(jnp.bfloat16)
    mid_own = solved_first[share:].astype(jnp.bfloat16)
    arrow_one = jnp.einsum(
        "ik,jk->ij",
        arrow_rows[0, 0],
        inverse_whole.astype(jnp.float32),
        precision=lax.Precision.HIGHEST,
    )
    top_whole, mid_whole = spread_panels(top_own, mid_own)
    sep_first = outer_rows(top_own, top_whole)
    fill_rows = -outer_rows(top_own, mid_whole)
    arrow_two_rows = arrow_rows[0, 1] - outer_rows(arrow_one.astype(jnp.bfloat16), mid_whole)
    tip_first = jnp.einsum("ik,jk->ij", arrow_one, arrow_one, precision=lax.Precision.HIGHEST)
    second_share = (second_diag[0].astype(jnp.float32) - outer_rows(mid_own, mid_whole)).astype(
        jnp.bfloat16
    )
    second_ready = gather_block(second_share)
    factor_two = jnp.linalg.cholesky(second_ready.astype(jnp.float32))
    rhs_second = jnp.concatenate(
        [fill_rows, coupling[0, 2].astype(jnp.float32), arrow_two_rows], axis=0
    )
    solved_second = right_solve(factor_two, rhs_second)
    upper_own = solved_second[:share].astype(jnp.bfloat16)
    lower_own = solved_second[share : 2 * share].astype(jnp.bfloat16)
    arrow_two = solved_second[2 * share :]
    tip_second = jnp.einsum("ik,jk->ij", arrow_two, arrow_two, precision=lax.Precision.HIGHEST)
    upper_whole, lower_whole = spread_panels(upper_own, lower_own)
    sep_second = outer_rows(upper_own, upper_whole)
    fill_block = -outer_rows(upper_own, lower_whole)
    handed = outer_rows(lower_own, lower_whole)
    incoming = from_behind(handed, "tm", 1)
    tip_total = lax.psum(tip_first + tip_second, "tm")
    separator_update = sep_first + sep_second + incoming
    return (separator_update[None], fill_block[None], tip_block - tip_total)


def solution(mesh):
    return jax.shard_map(
        shards,
        mesh=mesh,
        in_specs=(
            P("tm", ("row", "col"), None),
            P("tm", ("row", "col"), None),
            P("tm", None, ("row", "col"), None),
            P("tm", None, None, None),
            P(),
        ),
        out_specs=(P("tm", ("row", "col"), None), P("tm", ("row", "col"), None), P()),
        check_vma=False,
    )
```

profile of v0, /device:TPU:0, one launch (start us, length us, event | category | flops | bytes accessed | tf_op | source)
XLA Modules:
  0.0 1064.2 jit_solution(15958643128094356016)
XLA Ops:
  9.5 82.6 %all-gather.18.cloned.1.call-done = bf16[1,1536,1536]{2,1,0:T(8,128)(2,1)} async-done(((bf16[1,192,1536]{2,1,0:T(8,128)(2,1)}), bf16[1,1536,1536]{2,1,0:T(8,128)(2,1)}) %all-gather.18.cloned.1.call-update) | async-done | bytes 4718608 | tf_op jit(solution)/shard_map/all_gather | solution.py:24
  92.2 4.4 fusion.5
  97.7 77.8 %all-gather.10.cloned.1.call-done = bf16[1536,1536]{1,0:T(8,128)(2,1)} async-done(((bf16[192,1536]{1,0:T(8,128)(2,1)}), bf16[1536,1536]{1,0:T(8,128)(2,1)}) %all-gather.10.cloned.1.call-update) | async-done | bytes 4718608 | tf_op jit(solution)/shard_map/all_gather | solution.py:30
  175.5 4.8 fusion.11
  180.4 6.2 fusion.1
  191.3 66.9 %all-gather.12.cloned.1.call-done = bf16[1536,1536]{1,0:T(8,128)(2,1)} async-done(((bf16[192,1536]{1,0:T(8,128)(2,1)}), bf16[1536,1536]{1,0:T(8,128)(2,1)}) %all-gather.12.cloned.1.call-update) | async-done | bytes 4718608 | tf_op jit(solution)/shard_map/all_gather | solution.py:24
  258.2 6.6 copy.11
  264.8 7.9 copy.12
  272.8 6.5 fusion
  279.3 3.6 copy-done
  282.9 11.7 %cholesky.341 = f32[128,128]{1,0:T(8,128)S(1)} custom-call(f32[128,128]{1,0:T(8,128)S(1)} %cholesky.892), custom_call_target="Cholesky" | custom-call | tf_op jit(solution)/shard_map/jit(cholesky)/cholesky | solution.py:56
  294.7 9.8 custom-call.94
  304.5 4.8 cholesky.371
  314.0 11.9 %cholesky.362 = f32[128,128]{1,0:T(8,128)S(1)} custom-call(f32[128,128]{1,0:T(8,128)S(1)} %cholesky.896), custom_call_target="Cholesky" | custom-call | tf_op jit(solution)/shard_map/jit(cholesky)/cholesky | solution.py:56
  326.5 9.8 custom-call.95
  340.7 11.7 %cholesky.385 = f32[128,128]{1,0:T(8,128)S(1)} custom-call(f32[128,128]{1,0:T(8,128)S(1)} %cholesky.901), custom_call_target="Cholesky" | custom-call | tf_op jit(solution)/shard_map/jit(cholesky)/cholesky | solution.py:56
  353.7 9.8 custom-call.96
  365.2 3.3 convolution_subtract_fusion.1
  368.6 11.7 %cholesky.715 = f32[128,128]{1,0:T(8,128)S(1)} custom-call(f32[128,128]{1,0:T(8,128)S(1)} %cholesky.906), custom_call_target="Cholesky" | custom-call | tf_op jit(solution)/shard_map/jit(cholesky)/cholesky | solution.py:56
  381.6 9.8 custom-call.97
  392.9 3.6 fusion.28
  396.5 12.1 %cholesky.734 = f32[128,128]{1,0:T(8,128)S(1)} custom-call(f32[128,128]{1,0:T(8,128)S(1)} %cholesky.911), custom_call_target="Cholesky" | custom-call | tf_op jit(solution)/shard_map/jit(cholesky)/cholesky | solution.py:56
  409.9 9.8 custom-call.98
  421.1 3.8 fusion.31
  424.9 11.7 %cholesky.754 = f32[128,128]{1,0:T(8,128)S(1)} custom-call(f32[128,128]{1,0:T(8,128)S(1)} %cholesky.916), custom_call_target="Cholesky" | custom-call | tf_op jit(solution)/shard_map/jit(cholesky)/cholesky | solution.py:56
  438.0 9.9 custom-call.99
  449.2 3.8 fusion.34
  453.0 11.7 %cholesky.774 = f32[128,128]{1,0:T(8,128)S(1)} custom-call(f32[128,128]{1,0:T(8,128)S(1)} %cholesky.921), custom_call_target="Cholesky" | custom-call | tf_op jit(solution)/shard_map/jit(cholesky)/cholesky | solution.py:56
  466.1 9.8 custom-call.100
  477.1 3.8 fusion.37
  480.9 11.9 %cholesky.794 = f32[128,128]{1,0:T(8,128)S(1)} custom-call(f32[128,128]{1,0:T(8,128)S(1)} %cholesky.926), custom_call_target="Cholesky" | custom-call | tf_op jit(solution)/shard_map/jit(cholesky)/cholesky | solution.py:56
  494.2 9.8 custom-call.101
  505.1 3.6 fusion.43
  508.7 11.7 %cholesky.814 = f32[128,128]{1,0:T(8,128)S(1)} custom-call(f32[128,128]{1,0:T(8,128)S(1)} %cholesky.931), custom_call_target="Cholesky" | custom-call | tf_op jit(solution)/shard_map/jit(cholesky)/cholesky | solution.py:56
  521.7 10.2 custom-call.102
  533.0 3.3 fusion.46
  536.3 11.7 %cholesky.834 = f32[128,128]{1,0:T(8,128)S(1)} custom-call(f32[128,128]{1,0:T(8,128)S(1)} %cholesky.936), custom_call_target="Cholesky" | custom-call | tf_op jit(solution)/shard_map/jit(cholesky)/cholesky | solution.py:56
  549.3 9.8 custom-call.103
  562.9 11.9 %cholesky.854 = f32[128,128]{1,0:T(8,128)S(1)} custom-call(f32[128,128]{1,0:T(8,128)S(1)} %cholesky.941), custom_call_target="Cholesky" | custom-call | tf_op jit(solution)/shard_map/jit(cholesky)/cholesky | solution.py:56
  576.1 9.8 custom-call.104
  589.0 11.7 %cholesky.872 = f32[128,128]{1,0:T(8,128)S(1)} custom-call(f32[128,128]{1,0:T(8,128)S(1)} %convolution_subtract_fusion.16), custom_call_target="Cholesky" | custom-call | tf_op jit(solution)/shard_map/jit(cholesky)/cholesky | solution.py:56
  610.4 8.6 select_select_fusion
  619.0 43.1 %while.1 = (s32[]{:T(128)}, f32[1536,1536]{1,0:T(8,128)}, s32[12,2]{0,1:T(2,128)S(1)}, f32[12,128,128]{2,1,0:T(8,128)}, s32[]{:T(128)}) while((s32[]{:T(128)}, f32[1536,1536]{1,0:T(8,128)}, s32[12,2]{0,1:T(2,128)S(1)}, f32[12,128,128]{2,1,0:T(8,128)}, s32[]{:T(128)}) %tuple.111), condition=%wide.while_cond, body=%wide.while_body.sunk | while | flops 2 | bytes 132205 | solution.py:14
  619.7 2.9 bitcast_dynamic-update-slice_fusion.2
  623.3 2.9 bitcast_dynamic-update-slice_fusion.2
  626.9 2.9 bitcast_dynamic-update-slice_fusion.2
  630.5 2.9 bitcast_dynamic-update-slice_fusion.2
  634.0 2.9 bitcast_dynamic-update-slice_fusion.2
  637.6 2.9 bitcast_dynamic-update-slice_fusion.2
  641.2 2.9 bitcast_dynamic-update-slice_fusion.2
  644.8 2.9 bitcast_dynamic-update-slice_fusion.2
  648.4 2.9 bitcast_dynamic-update-slice_fusion.2
  652.0 2.9 bitcast_dynamic-update-slice_fusion.2
  655.6 2.9 bitcast_dynamic-update-slice_fusion.2
  662.1 119.7 %custom-call.105 = f32[12,128,128]{1,2,0:T(8,128)} custom-call(f32[12,128,128]{2,1,0:T(8,128)} %get-tuple-element.10), custom_call_target="InvertDiagBlocksLowerTriangular" | custom-call | tf_op jit(solution)/shard_map/triangular_solve | solution.py:14
  809.2 3.1 convolution_subtract_fusion.12
  815.8 76.7 %all-gather.16.cloned.1.call-done = bf16[1536,1536]{1,0:T(8,128)(2,1)} async-done(((bf16[192,1536]{1,0:T(8,128)(2,1)}), bf16[1536,1536]{1,0:T(8,128)(2,1)}) %all-gather.16.cloned.1.call-update) | async-done | bytes 4718608 | tf_op jit(solution)/shard_map/all_gather | solution.py:30
  892.5 5.0 fusion.132
  899.0 73.1 %all-gather.8.cloned.1.call-done = bf16[1536,1536]{1,0:T(8,128)(2,1)} async-done(((bf16[192,1536]{1,0:T(8,128)(2,1)}), bf16[1536,1536]{1,0:T(8,128)(2,1)}) %all-gather.8.cloned.1.call-update) | async-done | bytes 4718608 | tf_op jit(solution)/shard_map/all_gather | solution.py:29
  972.1 5.2 fusion.138
  978.4 5.7 psum.7
  984.7 5.0 fusion.8
  989.7 62.1 %all-gather.14.cloned.1.call-done = bf16[1536,1536]{1,0:T(8,128)(2,1)} async-done(((bf16[192,1536]{1,0:T(8,128)(2,1)}), bf16[1536,1536]{1,0:T(8,128)(2,1)}) %all-gather.14.cloned.1.call-update) | async-done | bytes 4718608 | tf_op jit(solution)/shard_map/all_gather | solution.py:29
  1051.8 5.4 fusion.10
  (140 shorter events, 92.6 us)
Async XLA Ops:
  7.2 85.0 %all-gather.18.cloned.1.call-start = ((), (), s32[]{:S(2)}) async-start(), calls=%async_computation.5 | async-start | bytes 5308416 | tf_op jit(solution)/shard_map/all_gather | solution.py:24
  7.9 167.6 %all-gather.10.cloned.1.call-start = ((), (), s32[]{:S(2)}) async-start(), calls=%async_computation.1 | async-start | bytes 5308416 | tf_op jit(solution)/shard_map/all_gather | solution.py:30
  96.5 91.5 %copy-start.4 = (bf16[384,1536]{1,0:T(8,128)(2,1)}, bf16[384,1536]{1,0:T(8,128)(2,1)S(1)}, u32[]{:S(2)}) copy-start(bf16[384,1536]{1,0:T(8,128)(2,1)S(1)} %fusion.5) | copy-start | bytes 3538948
  96.5 79.0 %copy-start.8 = (bf16[1,192,1536]{2,1,0:T(8,128)(2,1)S(1)}, bf16[1,192,1536]{2,1,0:T(8,128)(2,1)}, u32[]{:S(2)}) copy-start(bf16[1,192,1536]{2,1,0:T(8,128)(2,1)} %param.6) | copy-start | bytes 1769476
  97.7 82.8 %copy-start.6 = (f32[1,2,8,1536]{3,2,1,0:T(8,128)S(1)}, f32[1,2,8,1536]{3,2,1,0:T(8,128)}, u32[]{:S(2)}) copy-start(f32[1,2,8,1536]{3,2,1,0:T(8,128)} %param.8) | copy-start | bytes 294916
  97.7 160.5 %all-gather.12.cloned.1.call-start = ((), (), s32[]{:S(2)}) async-start(), calls=%async_computation.2 | async-start | bytes 5308416 | tf_op jit(solution)/shard_map/all_gather | solution.py:24
  180.4 712.1 %all-gather.16.cloned.1.call-start = ((), (), s32[]{:S(2)}) async-start(), calls=%async_computation.4 | async-start | bytes 5308416 | tf_op jit(solution)/shard_map/all_gather | solution.py:30
  180.4 6.2 copy-start.2
  279.3 3.6 copy-start
  610.4 171.4 %copy-start.1 = (f32[392,1536]{1,0:T(8,128)S(1)}, f32[392,1536]{1,0:T(8,128)}, u32[]{:S(2)}) copy-start(f32[392,1536]{1,0:T(8,128)} %pad_maximum_fusion) | copy-start | bytes 7225348
  781.8 2.8 copy-start.5
  812.8 1.8 copy-start.3
  814.6 157.5 %all-gather.8.cloned.1.call-start = ((), (), s32[]{:S(2)}) async-start(), calls=%async_computation | async-start | bytes 5308416 | tf_op jit(solution)/shard_map/all_gather | solution.py:29
  815.2 236.6 %all-gather.14.cloned.1.call-start = ((), (), s32[]{:S(2)}) async-start(), calls=%async_computation.3 | async-start | bytes 5308416 | tf_op jit(solution)/shard_map/all_gather | solution.py:29
  897.5 154.3 %collective-permute-start = (f32[192,1536]{1,0:T(8,128)}, f32[192,1536]{1,0:T(8,128)S(1)}, u32[]{:S(2)}, u32[]{:S(2)}) collective-permute-start(f32[192,1536]{1,0:T(8,128)} %fusion.132), channel_id=1, source_target_pairs={{0,8},{8,16},{16,24},{1,9},{9,17},{17,25},{2,10},{10,18},{18,26},{... | collective-permute-start | bytes 3538952 | tf_op jit(solution)/shard_map/ppermute | solution.py:10
  899.0 85.1 %copy-start.7 = (f32[8,8]{1,0:T(8,128)S(1)}, f32[8,8]{1,0:T(8,128)}, u32[]{:S(2)}) copy-start(f32[8,8]{1,0:T(8,128)} %param.9) | copy-start | bytes 772
Sparse Core Ops, SparseCore 0:
  10.1 82.0 all-gather.17
  97.8 77.6 all-gather.9
  180.5 77.6 all-gather.11
  814.7 77.6 all-gather.15
  894.4 77.6 all-gather.7
  974.1 77.6 all-gather.13
where the time goes:
time: 1070 us; the launch traced here: 1060 us
  waiting for transfers between devices  441 us (41%)
  other arithmetic  403 us (38%)
  matrix products  121 us (11%)
  local copies, waits for them, and re-layouts  68.9 us (6%)
  between operations  22.4 us (2%)
    another operation x46, other arithmetic, shards(): factor_two = jnp.linalg.cholesky(second_ready.astype(jnp.float32))  265 us
    all_gather x2, waiting for transfers between devices, spread_panels(): lax.all_gather(second_panel, ('row', 'col'), axis=0, tiled=True)  154 us
    all_gather x2, waiting for transfers between devices, gather_block(): return lax.all_gather(one_share, ('row', 'col'), axis=0, tiled=True)  150 us
    all_gather x2, waiting for transfers between devices, spread_panels(): lax.all_gather(first_panel, ('row', 'col'), axis=0, tiled=True)  135 us
    another operation x3, other arithmetic, right_solve(): lax.linalg.triangular_solve(factor, rhs_rows, left_side=False, lower=True...  128 us
    another operation x22, matrix products, shards(): factor_two = jnp.linalg.cholesky(second_ready.astype(jnp.float32))  50.1 us
    another operation x36, local copies, waits for them, and re-layouts  43 us
    dot_general x8, matrix products, outer_rows(): jnp.einsum('ik,jk->ij', left_rows, right_rows, preferred_element_type=jnp...  32.9 us
  transfers between devices with their start and end apart: 7, of which 6 were waited for; matrix products, arithmetic and copies ran while one was open for 3% of the time, Pallas kernels for 0%

commit v1 on v0

--- a/solution.py
+++ b/solution.py
@@ -2,6 +2,17 @@
 import jax.numpy as jnp
 from jax import lax
 from jax.sharding import PartitionSpec as P
+
+
+def ring_gather(array, axis, dim):
+    ways = lax.axis_size(axis)
+    pieces = [array]
+    for far in range(1, ways):
+        pieces.append(
+            lax.ppermute(pieces[far - 1], axis, [(d, (d - 1) % ways) for d in range(ways)])
+        )
+    line = jnp.concatenate(pieces, axis=dim)
+    return jnp.roll(line, lax.axis_index(axis) * array.shape[dim], axis=dim)
 
 
 def from_behind(block, axis, distance):
@@ -27,7 +38,7 @@
 def spread_panels(first_panel, second_panel):
     return (
         lax.all_gather(first_panel, ("row", "col"), axis=0, tiled=True),
-        lax.all_gather(second_panel, ("row", "col"), axis=0, tiled=True),
+        ring_gather(second_panel, ("row", "col"), 0),
     )
 
 

time: 1070 us -> 1070 us (level)
  waiting for transfers between devices: 441 us -> 352 us
  starting transfers between devices: 1.59 us -> 54 us
  local copies, waits for them, and re-layouts: 68.9 us -> 86.4 us
  other arithmetic: 403 us -> 419 us
    ppermute x0 -> x14, waiting for transfers between devices: none -> 199 us  [ring_gather(): lax.ppermute(pieces[far - 1], axis, [(d, (d - 1) % ways) for d in range(w...]
    all_gather x2 -> x0, waiting for transfers between devices: 154 us -> none  [spread_panels(): lax.all_gather(second_panel, ('row', 'col'), axis=0, tiled=True)]
    all_gather x2, waiting for transfers between devices: 135 us -> 0.02 us  [spread_panels(): lax.all_gather(first_panel, ('row', 'col'), axis=0, tiled=True)]
    ppermute x0 -> x14, starting transfers between devices: none -> 51.9 us  [ring_gather(): lax.ppermute(pieces[far - 1], axis, [(d, (d - 1) % ways) for d in range(w...]
    unnamed x18 -> x38, local copies, waits for them, and re-layouts: 3.96 us -> 19.5 us
    concatenate x0 -> x2, other arithmetic: none -> 14.2 us  [ring_gather(): return jnp.roll(line, lax.axis_index(axis) * array.shape[dim], axis=dim)]
  transfers between devices with their start and end apart: 7 -> 19, of which waited for: 6 -> 16; matrix products, arithmetic and copies ran while one was open for 3% -> 56% of each run, Pallas kernels for 0% -> 0%
where the time goes in v1:
time: 1070 us; the launch traced here: 1060 us
  other arithmetic  419 us (39%)
  waiting for transfers between devices  352 us (33%)
  matrix products  116 us (11%)
  local copies, waits for them, and re-layouts  86.4 us (8%)
  starting transfers between devices  54 us (5%)
  between operations  22.1 us (2%)
    another operation x46, other arithmetic, shards(): factor_two = jnp.linalg.cholesky(second_ready.astype(jnp.float32))  265 us
    ppermute x14, waiting for transfers between devices, ring_gather(): lax.ppermute(pieces[far - 1], axis, [(d, (d - 1) % ways) for d in range(w...  199 us
    all_gather x2, waiting for transfers between devices, gather_block(): return lax.all_gather(one_share, ('row', 'col'), axis=0, tiled=True)  152 us
    another operation x3, other arithmetic, right_solve(): lax.linalg.triangular_solve(factor, rhs_rows, left_side=False, lower=True...  128 us
    ppermute x14, starting transfers between devices, ring_gather(): lax.ppermute(pieces[far - 1], axis, [(d, (d - 1) % ways) for d in range(w...  51.9 us
    another operation x22, matrix products, shards(): factor_two = jnp.linalg.cholesky(second_ready.astype(jnp.float32))  50.1 us
    another operation x36, local copies, waits for them, and re-layouts  43 us
    another operation x23, matrix products, right_solve(): lax.linalg.triangular_solve(factor, rhs_rows, left_side=False, lower=True...  31.1 us
  transfers between devices with their start and end apart: 19, of which 16 were waited for; matrix products, arithmetic and copies ran while one was open for 56% of the time, Pallas kernels for 0%

profile of v1, /device:TPU:0, one launch (start us, length us, event | category | flops | bytes accessed | tf_op | source)
XLA Modules:
  0.0 1056.5 jit_solution(4094758188513718265)
XLA Ops:
  9.5 82.6 %all-gather.12.cloned.1.call-done = bf16[1,1536,1536]{2,1,0:T(8,128)(2,1)} async-done(((bf16[1,192,1536]{2,1,0:T(8,128)(2,1)}), bf16[1,1536,1536]{2,1,0:T(8,128)(2,1)}) %all-gather.12.cloned.1.call-update) | async-done | bytes 4718608 | tf_op jit(solution)/shard_map/all_gather | solution.py:35
  92.2 4.4 fusion.7
  99.5 12.6 %collective-permute-done = bf16[192,1536]{1,0:T(8,128)(2,1)S(1)} collective-permute-done((bf16[192,1536]{1,0:T(8,128)(2,1)S(1)}, bf16[192,1536]{1,0:T(8,128)(2,1)S(1)}, u32[]{:S(2)}, u32[]{:S(2)}) %collective-permute-start) | collective-permute-done | bytes 589856 | tf_op jit(solution)/shard_map/ppermute | solution.py:12
  112.1 5.2 collective-permute-start.1
  117.3 11.8 %collective-permute-done.1 = bf16[192,1536]{1,0:T(8,128)(2,1)S(1)} collective-permute-done((bf16[192,1536]{1,0:T(8,128)(2,1)S(1)}, bf16[192,1536]{1,0:T(8,128)(2,1)S(1)}, u32[]{:S(2)}, u32[]{:S(2)}) %collective-permute-start.1) | collective-permute-done | bytes 589856 | tf_op jit(solution)/shard_map/ppermute | solution.py:12
  129.0 5.2 collective-permute-start.2
  134.2 10.9 %collective-permute-done.2 = bf16[192,1536]{1,0:T(8,128)(2,1)S(1)} collective-permute-done((bf16[192,1536]{1,0:T(8,128)(2,1)S(1)}, bf16[192,1536]{1,0:T(8,128)(2,1)S(1)}, u32[]{:S(2)}, u32[]{:S(2)}) %collective-permute-start.2) | collective-permute-done | bytes 589856 | tf_op jit(solution)/shard_map/ppermute | solution.py:12
  145.9 5.2 collective-permute-start.3
  151.1 10.0 collective-permute-done.3
  161.1 5.3 collective-permute-start.4
  166.4 9.5 collective-permute-done.4
  175.9 5.2 collective-permute-start.5
  183.7 6.1 collective-permute-done.5
  189.8 5.1 collective-permute-start.6
  203.2 7.1 fusion.2
  216.4 6.2 fusion.3
  227.3 69.0 %all-gather.8.cloned.1.call-done = bf16[1536,1536]{1,0:T(8,128)(2,1)} async-done(((bf16[192,1536]{1,0:T(8,128)(2,1)}), bf16[1536,1536]{1,0:T(8,128)(2,1)}) %all-gather.8.cloned.1.call-update) | async-done | bytes 4718608 | tf_op jit(solution)/shard_map/all_gather | solution.py:35
  296.3 6.6 copy.11
  302.9 7.7 copy.12
  310.6 6.5 fusion
  320.8 11.7 %cholesky.341 = f32[128,128]{1,0:T(8,128)S(1)} custom-call(f32[128,128]{1,0:T(8,128)S(1)} %cholesky.892), custom_call_target="Cholesky" | custom-call | tf_op jit(solution)/shard_map/jit(cholesky)/cholesky | solution.py:67
  332.5 9.8 custom-call.94
  342.3 4.8 cholesky.371
  351.8 11.9 %cholesky.362 = f32[128,128]{1,0:T(8,128)S(1)} custom-call(f32[128,128]{1,0:T(8,128)S(1)} %cholesky.896), custom_call_target="Cholesky" | custom-call | tf_op jit(solution)/shard_map/jit(cholesky)/cholesky | solution.py:67
  364.4 9.8 custom-call.95
  378.5 11.7 %cholesky.385 = f32[128,128]{1,0:T(8,128)S(1)} custom-call(f32[128,128]{1,0:T(8,128)S(1)} %cholesky.901), custom_call_target="Cholesky" | custom-call | tf_op jit(solution)/shard_map/jit(cholesky)/cholesky | solution.py:67
  391.5 9.8 custom-call.96
  406.4 11.7 %cholesky.715 = f32[128,128]{1,0:T(8,128)S(1)} custom-call(f32[128,128]{1,0:T(8,128)S(1)} %cholesky.906), custom_call_target="Cholesky" | custom-call | tf_op jit(solution)/shard_map/jit(cholesky)/cholesky | solution.py:67
  419.4 9.8 custom-call.97
  434.3 12.1 %cholesky.734 = f32[128,128]{1,0:T(8,128)S(1)} custom-call(f32[128,128]{1,0:T(8,128)S(1)} %cholesky.911), custom_call_target="Cholesky" | custom-call | tf_op jit(solution)/shard_map/jit(cholesky)/cholesky | solution.py:67
  447.6 9.8 custom-call.98
  458.8 3.8 fusion.31
  462.7 11.7 %cholesky.754 = f32[128,128]{1,0:T(8,128)S(1)} custom-call(f32[128,128]{1,0:T(8,128)S(1)} %cholesky.916), custom_call_target="Cholesky" | custom-call | tf_op jit(solution)/shard_map/jit(cholesky)/cholesky | solution.py:67
  475.8 9.9 custom-call.99
  487.0 3.8 fusion.34
  490.8 11.7 %cholesky.774 = f32[128,128]{1,0:T(8,128)S(1)} custom-call(f32[128,128]{1,0:T(8,128)S(1)} %cholesky.921), custom_call_target="Cholesky" | custom-call | tf_op jit(solution)/shard_map/jit(cholesky)/cholesky | solution.py:67
  503.9 9.8 custom-call.100
  518.7 11.9 %cholesky.794 = f32[128,128]{1,0:T(8,128)S(1)} custom-call(f32[128,128]{1,0:T(8,128)S(1)} %cholesky.926), custom_call_target="Cholesky" | custom-call | tf_op jit(solution)/shard_map/jit(cholesky)/cholesky | solution.py:67
  532.0 9.8 custom-call.101
  546.5 11.7 %cholesky.814 = f32[128,128]{1,0:T(8,128)S(1)} custom-call(f32[128,128]{1,0:T(8,128)S(1)} %cholesky.931), custom_call_target="Cholesky" | custom-call | tf_op jit(solution)/shard_map/jit(cholesky)/cholesky | solution.py:67
  559.5 10.2 custom-call.102
  574.1 11.7 %cholesky.834 = f32[128,128]{1,0:T(8,128)S(1)} custom-call(f32[128,128]{1,0:T(8,128)S(1)} %cholesky.936), custom_call_target="Cholesky" | custom-call | tf_op jit(solution)/shard_map/jit(cholesky)/cholesky | solution.py:67
  587.1 9.8 custom-call.103
  600.7 11.9 %cholesky.854 = f32[128,128]{1,0:T(8,128)S(1)} custom-call(f32[128,128]{1,0:T(8,128)S(1)} %cholesky.941), custom_call_target="Cholesky" | custom-call | tf_op jit(solution)/shard_map/jit(cholesky)/cholesky | solution.py:67
  613.9 9.8 custom-call.104
  626.9 11.7 %cholesky.872 = f32[128,128]{1,0:T(8,128)S(1)} custom-call(f32[128,128]{1,0:T(8,128)S(1)} %convolution_subtract_fusion.5), custom_call_target="Cholesky" | custom-call | tf_op jit(solution)/shard_map/jit(cholesky)/cholesky | solution.py:67
  648.1 8.6 select_select_fusion
  656.8 43.1 %while.1 = (s32[]{:T(128)}, f32[1536,1536]{1,0:T(8,128)}, s32[12,2]{0,1:T(2,128)S(1)}, f32[12,128,128]{2,1,0:T(8,128)}, s32[]{:T(128)}) while((s32[]{:T(128)}, f32[1536,1536]{1,0:T(8,128)}, s32[12,2]{0,1:T(2,128)S(1)}, f32[12,128,128]{2,1,0:T(8,128)}, s32[]{:T(128)}) %tuple.114), condition=%wide.while_cond, body=%wide.while_body.sunk | while | flops 2 | bytes 132205 | solution.py:25
  699.8 119.5 %custom-call.105 = f32[12,128,128]{1,2,0:T(8,128)} custom-call(f32[12,128,128]{2,1,0:T(8,128)} %get-tuple-element.11), custom_call_target="InvertDiagBlocksLowerTriangular" | custom-call | tf_op jit(solution)/shard_map/triangular_solve | solution.py:25
  854.1 25.4 %collective-permute-done.7 = bf16[192,1536]{1,0:T(8,128)(2,1)S(1)} collective-permute-done((bf16[192,1536]{1,0:T(8,128)(2,1)S(1)}, bf16[192,1536]{1,0:T(8,128)(2,1)S(1)}, u32[]{:S(2)}, u32[]{:S(2)}) %collective-permute-start.7) | collective-permute-done | bytes 589856 | tf_op jit(solution)/shard_map/ppermute | solution.py:12
  879.8 18.5 %collective-permute-done.8 = bf16[192,1536]{1,0:T(8,128)(2,1)S(1)} collective-permute-done((bf16[192,1536]{1,0:T(8,128)(2,1)S(1)}, bf16[192,1536]{1,0:T(8,128)(2,1)S(1)}, u32[]{:S(2)}, u32[]{:S(2)}) %collective-permute-start.8) | collective-permute-done | bytes 589856 | tf_op jit(solution)/shard_map/ppermute | solution.py:12
  898.3 5.2 collective-permute-start.9
  903.5 27.9 %collective-permute-done.9 = bf16[192,1536]{1,0:T(8,128)(2,1)S(1)} collective-permute-done((bf16[192,1536]{1,0:T(8,128)(2,1)S(1)}, bf16[192,1536]{1,0:T(8,128)(2,1)S(1)}, u32[]{:S(2)}, u32[]{:S(2)}) %collective-permute-start.9) | collective-permute-done | bytes 589856 | tf_op jit(solution)/shard_map/ppermute | solution.py:12
  932.9 29.9 %collective-permute-done.10 = bf16[192,1536]{1,0:T(8,128)(2,1)S(1)} collective-permute-done((bf16[192,1536]{1,0:T(8,128)(2,1)S(1)}, bf16[192,1536]{1,0:T(8,128)(2,1)S(1)}, u32[]{:S(2)}, u32[]{:S(2)}) %collective-permute-start.10) | collective-permute-done | bytes 589856 | tf_op jit(solution)/shard_map/ppermute | solution.py:12
  963.0 15.3 %collective-permute-done.11 = bf16[192,1536]{1,0:T(8,128)(2,1)S(1)} collective-permute-done((bf16[192,1536]{1,0:T(8,128)(2,1)S(1)}, bf16[192,1536]{1,0:T(8,128)(2,1)S(1)}, u32[]{:S(2)}, u32[]{:S(2)}) %collective-permute-start.11) | collective-permute-done | bytes 589856 | tf_op jit(solution)/shard_map/ppermute | solution.py:12
  978.3 5.2 collective-permute-start.12
  986.0 9.5 collective-permute-done.12
  995.5 5.3 collective-permute-start.13
  1003.5 8.6 collective-permute-done.13
  1013.1 7.0 fusion.1
  1024.4 5.2 fusion.149
  1030.7 7.9 psum.7
  1039.2 5.0 fusion.10
  1044.3 4.4 convolution_add_fusion
  (187 shorter events, 181.4 us)
Async XLA Ops:
  7.2 85.0 %all-gather.12.cloned.1.call-start = ((), (), s32[]{:S(2)}) async-start(), calls=%async_computation.3 | async-start | bytes 5308416 | tf_op jit(solution)/shard_map/all_gather | solution.py:35
  7.9 288.4 %all-gather.8.cloned.1.call-start = ((), (), s32[]{:S(2)}) async-start(), calls=%async_computation.1 | async-start | bytes 5308416 | tf_op jit(solution)/shard_map/all_gather | solution.py:35
  96.5 126.1 %copy-start.6 = (bf16[384,1536]{1,0:T(8,128)(2,1)}, bf16[384,1536]{1,0:T(8,128)(2,1)S(1)}, u32[]{:S(2)}) copy-start(bf16[384,1536]{1,0:T(8,128)(2,1)S(1)} %fusion.7) | copy-start | bytes 3538948
  97.8 14.3 %collective-permute-start = (bf16[192,1536]{1,0:T(8,128)(2,1)S(1)}, bf16[192,1536]{1,0:T(8,128)(2,1)S(1)}, u32[]{:S(2)}, u32[]{:S(2)}) collective-permute-start(bf16[192,1536]{1,0:T(8,128)(2,1)S(1)} %get-tuple-element.28), channel_id=1, source_target_pairs={{0,7},{1,0},{2,1},{3,2},{4,3},{5,4},{6,5},{7,6},{8,15},{9,8},{10,9... | collective-permute-start | bytes 1769480 | tf_op jit(solution)/shard_map/ppermute | solution.py:12
  112.1 16.9 %collective-permute-start.1 = (bf16[192,1536]{1,0:T(8,128)(2,1)S(1)}, bf16[192,1536]{1,0:T(8,128)(2,1)S(1)}, u32[]{:S(2)}, u32[]{:S(2)}) collective-permute-start(bf16[192,1536]{1,0:T(8,128)(2,1)S(1)} %collective-permute-done), channel_id=1, source_target_pairs={{0,7},{1,0},{2,1},{3,2},{4,3},{5,4},{6,5},{7,6},{8,15},{9,8},{10,9... | collective-permute-start | bytes 1769480 | tf_op jit(solution)/shard_map/ppermute | solution.py:12
  129.0 16.1 %collective-permute-start.2 = (bf16[192,1536]{1,0:T(8,128)(2,1)S(1)}, bf16[192,1536]{1,0:T(8,128)(2,1)S(1)}, u32[]{:S(2)}, u32[]{:S(2)}) collective-permute-start(bf16[192,1536]{1,0:T(8,128)(2,1)S(1)} %collective-permute-done.1), channel_id=1, source_target_pairs={{0,7},{1,0},{2,1},{3,2},{4,3},{5,4},{6,5},{7,6},{8,15},{9,8},{10,9... | collective-permute-start | bytes 1769480 | tf_op jit(solution)/shard_map/ppermute | solution.py:12
  145.1 0.8 copy-start.8
  145.9 15.2 %collective-permute-start.3 = (bf16[192,1536]{1,0:T(8,128)(2,1)S(1)}, bf16[192,1536]{1,0:T(8,128)(2,1)}, u32[]{:S(2)}, u32[]{:S(2)}) collective-permute-start(bf16[192,1536]{1,0:T(8,128)(2,1)S(1)} %collective-permute-done.2), channel_id=1, source_target_pairs={{0,7},{1,0},{2,1},{3,2},{4,3},{5,4},{6,5},{7,6},{8,15},{9,8},{10,9... | collective-permute-start | bytes 1769480 | tf_op jit(solution)/shard_map/ppermute | solution.py:12
  161.1 14.8 %collective-permute-start.4 = (bf16[192,1536]{1,0:T(8,128)(2,1)}, bf16[192,1536]{1,0:T(8,128)(2,1)}, u32[]{:S(2)}, u32[]{:S(2)}) collective-permute-start(bf16[192,1536]{1,0:T(8,128)(2,1)} %collective-permute-done.3), channel_id=1, source_target_pairs={{0,7},{1,0},{2,1},{3,2},{4,3},{5,4},{6,5},{7,6},{8,15},{9,8},{10,9... | collective-permute-start | bytes 1769480 | tf_op jit(solution)/shard_map/ppermute | solution.py:12
  166.4 16.4 %copy-start.9 = (bf16[192,1536]{1,0:T(8,128)(2,1)S(1)}, bf16[192,1536]{1,0:T(8,128)(2,1)}, u32[]{:S(2)}) copy-start(bf16[192,1536]{1,0:T(8,128)(2,1)} %copy-done.8) | copy-start | bytes 1769476
  175.9 13.8 %collective-permute-start.5 = (bf16[192,1536]{1,0:T(8,128)(2,1)}, bf16[192,1536]{1,0:T(8,128)(2,1)S(1)}, u32[]{:S(2)}, u32[]{:S(2)}) collective-permute-start(bf16[192,1536]{1,0:T(8,128)(2,1)} %collective-permute-done.4), channel_id=1, source_target_pairs={{0,7},{1,0},{2,1},{3,2},{4,3},{5,4},{6,5},{7,6},{8,15},{9,8},{10,9... | collective-permute-start | bytes 1769480 | tf_op jit(solution)/shard_map/ppermute | solution.py:12
  189.8 12.5 %collective-permute-start.6 = (bf16[192,1536]{1,0:T(8,128)(2,1)S(1)}, bf16[192,1536]{1,0:T(8,128)(2,1)S(1)}, u32[]{:S(2)}, u32[]{:S(2)}) collective-permute-start(bf16[192,1536]{1,0:T(8,128)(2,1)S(1)} %collective-permute-done.5), channel_id=1, source_target_pairs={{0,7},{1,0},{2,1},{3,2},{4,3},{5,4},{6,5},{7,6},{8,15},{9,8},{10,9... | collective-permute-start | bytes 1769480 | tf_op jit(solution)/shard_map/ppermute | solution.py:12
  203.2 9.4 copy-start.12
  210.4 2.2 copy-start.1
  212.6 3.8 copy-start.10
  215.1 809.3 %all-gather.6.cloned.1.call-start = ((), (), s32[]{:S(2)}) async-start(), calls=%async_computation | async-start | bytes 5308416 | tf_op jit(solution)/shard_map/all_gather | solution.py:40
  215.8 828.4 %all-gather.10.cloned.1.call-start = ((), (), s32[]{:S(2)}) async-start(), calls=%async_computation.2 | async-start | bytes 5308416 | tf_op jit(solution)/shard_map/all_gather | solution.py:40
  216.4 6.2 copy-start.2
  317.1 3.6 copy-start
  648.1 171.2 %copy-start.3 = (f32[392,1536]{1,0:T(8,128)S(1)}, f32[392,1536]{1,0:T(8,128)}, u32[]{:S(2)}) copy-start(f32[392,1536]{1,0:T(8,128)} %pad_maximum_fusion) | copy-start | bytes 7225348
  819.3 2.8 copy-start.7
  850.6 1.8 copy-start.5
  852.4 27.1 %collective-permute-start.7 = (bf16[192,1536]{1,0:T(8,128)(2,1)S(1)}, bf16[192,1536]{1,0:T(8,128)(2,1)S(1)}, u32[]{:S(2)}, u32[]{:S(2)}) collective-permute-start(bf16[192,1536]{1,0:T(8,128)(2,1)S(1)} %get-tuple-element.25), channel_id=1, source_target_pairs={{0,7},{1,0},{2,1},{3,2},{4,3},{5,4},{6,5},{7,6},{8,15},{9,8},{10,9... | collective-permute-start | bytes 1769480 | tf_op jit(solution)/shard_map/ppermute | solution.py:12
  879.6 18.7 %collective-permute-start.8 = (bf16[192,1536]{1,0:T(8,128)(2,1)S(1)}, bf16[192,1536]{1,0:T(8,128)(2,1)S(1)}, u32[]{:S(2)}, u32[]{:S(2)}) collective-permute-start(bf16[192,1536]{1,0:T(8,128)(2,1)S(1)} %collective-permute-done.7), channel_id=1, source_target_pairs={{0,7},{1,0},{2,1},{3,2},{4,3},{5,4},{6,5},{7,6},{8,15},{9,8},{10,9... | collective-permute-start | bytes 1769480 | tf_op jit(solution)/shard_map/ppermute | solution.py:12
  898.3 33.1 %collective-permute-start.9 = (bf16[192,1536]{1,0:T(8,128)(2,1)S(1)}, bf16[192,1536]{1,0:T(8,128)(2,1)S(1)}, u32[]{:S(2)}, u32[]{:S(2)}) collective-permute-start(bf16[192,1536]{1,0:T(8,128)(2,1)S(1)} %collective-permute-done.8), channel_id=1, source_target_pairs={{0,7},{1,0},{2,1},{3,2},{4,3},{5,4},{6,5},{7,6},{8,15},{9,8},{10,9... | collective-permute-start | bytes 1769480 | tf_op jit(solution)/shard_map/ppermute | solution.py:12
  931.4 31.4 %collective-permute-start.10 = (bf16[192,1536]{1,0:T(8,128)(2,1)S(1)}, bf16[192,1536]{1,0:T(8,128)(2,1)S(1)}, u32[]{:S(2)}, u32[]{:S(2)}) collective-permute-start(bf16[192,1536]{1,0:T(8,128)(2,1)S(1)} %collective-permute-done.9), channel_id=1, source_target_pairs={{0,7},{1,0},{2,1},{3,2},{4,3},{5,4},{6,5},{7,6},{8,15},{9,8},{10,9... | collective-permute-start | bytes 1769480 | tf_op jit(solution)/shard_map/ppermute | solution.py:12
  962.8 15.4 %collective-permute-start.11 = (bf16[192,1536]{1,0:T(8,128)(2,1)S(1)}, bf16[192,1536]{1,0:T(8,128)(2,1)S(1)}, u32[]{:S(2)}, u32[]{:S(2)}) collective-permute-start(bf16[192,1536]{1,0:T(8,128)(2,1)S(1)} %collective-permute-done.10), channel_id=1, source_target_pairs={{0,7},{1,0},{2,1},{3,2},{4,3},{5,4},{6,5},{7,6},{8,15},{9,8},{10,9... | collective-permute-start | bytes 1769480 | tf_op jit(solution)/shard_map/ppermute | solution.py:12
  978.3 17.3 %collective-permute-start.12 = (bf16[192,1536]{1,0:T(8,128)(2,1)S(1)}, bf16[192,1536]{1,0:T(8,128)(2,1)S(1)}, u32[]{:S(2)}, u32[]{:S(2)}) collective-permute-start(bf16[192,1536]{1,0:T(8,128)(2,1)S(1)} %collective-permute-done.11), channel_id=1, source_target_pairs={{0,7},{1,0},{2,1},{3,2},{4,3},{5,4},{6,5},{7,6},{8,15},{9,8},{10,9... | collective-permute-start | bytes 1769480 | tf_op jit(solution)/shard_map/ppermute | solution.py:12
  995.5 16.6 %collective-permute-start.13 = (bf16[192,1536]{1,0:T(8,128)(2,1)S(1)}, bf16[192,1536]{1,0:T(8,128)(2,1)S(1)}, u32[]{:S(2)}, u32[]{:S(2)}) collective-permute-start(bf16[192,1536]{1,0:T(8,128)(2,1)S(1)} %collective-permute-done.12), channel_id=1, source_target_pairs={{0,7},{1,0},{2,1},{3,2},{4,3},{5,4},{6,5},{7,6},{8,15},{9,8},{10,9... | collective-permute-start | bytes 1769480 | tf_op jit(solution)/shard_map/ppermute | solution.py:12
  1020.1 2.7 copy-start.4
  1022.9 15.8 %copy-start.11 = (f32[8,8]{1,0:T(8,128)S(1)}, f32[8,8]{1,0:T(8,128)}, u32[]{:S(2)}) copy-start(f32[8,8]{1,0:T(8,128)} %param.11) | copy-start | bytes 772
  1022.9 25.8 %collective-permute-start.14 = (f32[192,1536]{1,0:T(8,128)}, f32[192,1536]{1,0:T(8,128)S(1)}, u32[]{:S(2)}, u32[]{:S(2)}) collective-permute-start(f32[192,1536]{1,0:T(8,128)} %fusion.143), channel_id=1, source_target_pairs={{0,8},{8,16},{16,24},{1,9},{9,17},{17,25},{2,10},{10,18},{18,26},{... | collective-permute-start | bytes 3538952 | tf_op jit(solution)/shard_map/ppermute | solution.py:21
Sparse Core Ops, SparseCore 0:
  10.1 82.0 all-gather.11
  215.2 80.9 all-gather.7
  298.4 77.2 all-gather.5
  852.6 116.3 all-gather.9
